TPU v7x, 256 devices: a whole 4x4x8 slice. The times are simulated.
256 devices in a mesh: bank: 64 (over x_hi, z, y), tp: 4 (over x_lo, core).
Axes of the slice: x: 4 (x_hi: 2, x_lo: 2; x = x_hi * 2 + x_lo), y: 4, z: 8, core: 2. Of those that a mesh axis runs over, the one named last changes fastest.
Arguments:
- hidden: bfloat16 [128, 512, 14336], P('bank', None, 'tp'), may hold values from -6 to 6
- out_grad: bfloat16 [128, 512, 4096], P('bank', None, 'tp'), may hold values from -6 to 6
- proj_in: bfloat16 [64, 14336], P(None, 'tp'), may hold values from -0.046875 to 0.046875
- proj_out: bfloat16 [64, 4096], P(None, 'tp'), may hold values from -0.09375 to 0.09375
- lengths: int32 [128], P('bank'), may hold values from 1 to 512, 49152 in all
- pair_perm: int32 [128], replicated, may hold values from 0 to 127, each once
- bank_slab: bfloat16 [65536, 4096], P('bank', 'tp'), may hold values from -6 to 6
Outputs:
- scores: float32 [64, 65536], P('tp', 'bank')
Inputs may be any that keep to these rules, and one draw needn't show every extreme that they name: pair_perm holds every variant index exactly once. `lengths`: some prompt fills all 512 slots.
All inputs are finite; a program needn't handle non-finite values. No bound on the sum of `lengths` on one device may be relied on, other than what follows from the above.
Results may differ from a plain program's by a relative error of at most 0.0029.
Values sent between devices are 32-bit elements; how exact they have to be, the bound alone decides.
A program may use at most 64 MiB of HBM per device.

v0:
```python
import jax
import jax.numpy as jnp
from jax import lax
from jax.sharding import PartitionSpec as P

epsilon = 1e-06


def per_device(hidden, out_grad, proj_in, proj_out, lengths, pair_perm, bank_slab):
    ex_dev, seq_len, ff_dev = hidden.shape
    factor_rank = proj_in.shape[0]
    tp_count = lax.axis_size("tp")
    share_rows = factor_rank // tp_count
    tok_rows = hidden.reshape(ex_dev * seq_len, ff_dev)
    grad_rows = out_grad.reshape(ex_dev * seq_len, out_grad.shape[2])
    in_part = jnp.einsum("rf,tf->rt", proj_in, tok_rows, preferred_element_type=jnp.float32)
    out_part = jnp.einsum("rd,td->rt", proj_out, grad_rows, preferred_element_type=jnp.float32)
    in_all, out_all = lax.psum((in_part, out_part), "tp")
    in_mine = lax.dynamic_slice_in_dim(in_all, lax.axis_index("tp") * share_rows, share_rows, 0)
    positions = jnp.arange(seq_len, dtype=jnp.int32)
    live_mask = (positions[None, :] < lengths[:, None]).astype(jnp.float32)
    in_three = in_mine.reshape(share_rows, ex_dev, seq_len) * live_mask[None, :, :]
    out_three = out_all.reshape(factor_rank, ex_dev, seq_len)
    grads = jnp.einsum("ies,jes->eij", in_three, out_three, precision=lax.Precision.HIGHEST)
    grads = grads.reshape(ex_dev, share_rows * factor_rank)
    benign = pair_perm[0::2]
    harmful = pair_perm[1::2]
    all_grads = lax.all_gather(grads, "bank", axis=0, tiled=True)
    example_ids = jnp.arange(all_grads.shape[0], dtype=jnp.int32)
    pair_signs = (example_ids[None, :] == harmful[:, None]).astype(jnp.float32) - (
        example_ids[None, :] == benign[:, None]
    ).astype(jnp.float32)
    queries = jnp.dot(pair_signs, all_grads, precision=lax.Precision.HIGHEST)
    query_part = jnp.sum(queries * queries, axis=1)
    slab_wide = bank_slab.astype(jnp.float32)
    bank_part = jnp.sum(slab_wide * slab_wide, axis=1)
    query_sq, bank_sq = lax.psum((query_part, bank_part), "tp")
    query_low = queries.astype(jnp.bfloat16)
    pair_count = queries.shape[0]
    pairs_mine = pair_count // tp_count
    dots = lax.psum_scatter(
        lax.dot_general(
            query_low, bank_slab, (((1,), (1,)), ((), ())), preferred_element_type=jnp.float32
        ),
        "tp",
        scatter_dimension=0,
        tiled=True,
    )
    query_mine = lax.dynamic_slice_in_dim(
        query_sq, lax.axis_index("tp") * pairs_mine, pairs_mine, 0
    )
    return (
        dots
        * factor_rank
        * lax.rsqrt(query_mine + epsilon)[:, None]
        * lax.rsqrt(bank_sq + epsilon)[None, :]
    )


def solution(mesh):
    return jax.shard_map(
        per_device,
        mesh=mesh,
        in_specs=(
            P("bank", None, "tp"),
            P("bank", None, "tp"),
            P(None, "tp"),
            P(None, "tp"),
            P("bank"),
            P(),
            P("bank", "tp"),
        ),
        out_specs=P("tp", "bank"),
        check_vma=False,
    )
```

profile of v0, /device:TPU:1, one launch (start us, length us, event | category | flops | bytes accessed | tf_op | source)
XLA Modules:
  0.0 274.3 jit_solution(10950495381931768916)
XLA Ops:
  6.5 0.0 copy-start
  6.5 0.0 copy-start.1
  6.5 0.0 all-reduce.4.cloned.1.call-start
  6.5 1.6 copy-done
  8.1 1.7 fusion.11
  9.8 0.7 copy.17
  10.5 0.0 copy-done.1
  10.5 0.0 copy-start.3
  10.5 0.0 copy-start.2
  10.5 6.1 %fusion.10 = f32[64,1024]{1,0:T(8,128)} fusion(bf16[64,3584]{1,0:T(8,128)(2,1)S(1)} %copy-done.1, bf16[1024,3584]{1,0:T(8,128)(2,1)} %bitcast.18), kind=kOutput, calls=%fused_computation.21 | convolution fusion | flops 469762048 | bytes 8060928 | tf_op jit(solution)/shard_map/rf,tf->rt/dot_general | solution.py:16
  16.6 0.0 all-reduce.4.cloned.1.call-update
  16.7 0.0 reduce-scatter.2.cloned.1.call-start
  16.7 0.0 copy-done.3
  16.7 0.2 slice.7
  16.9 0.2 slice.6
  17.1 0.0 copy-done.2
  17.1 0.1 compare_convert_fusion
  17.1 46.7 %all-reduce.4.cloned.1.call-done = (f32[64,2,512]{2,0,1:T(8,128)}, f32[64,1024]{1,0:T(8,128)}) async-done(((f32[64,2,512]{2,0,1:T(8,128)}, f32[64,1024]{1,0:T(8,128)}), (f32[64,2,512]{2,0,1:T(8,128)}, f32[64,1024]{1,0:T(8,128)})) %all-reduce.4.cloned.1.call-update) | async-done | bytes 524304 | tf_op jit(solution)/shard_map/psum | solution.py:18
  63.9 0.8 constant_dynamic-slice_fusion
  64.7 0.1 reshape.39
  64.8 1.3 fusion.2
  66.1 0.1 reshape.43
  66.2 156.8 %all-gather = f32[64,2,1024]{2,1,0:T(2,128)S(1)} all-gather(f32[1,2,1024]{2,1,0:T(2,128)S(1)} %reshape.43), channel_id=1, replica_groups=mesh['bank'=64,'tp'=4] {'bank'}, dimensions={0}, use_global_device_ids=true | all-gather | bytes 532480 | tf_op jit(solution)/shard_map/all_gather | solution.py:28
  223.0 0.4 reshape.44
  223.3 0.5 multiply_reduce_fusion.1
  223.9 3.0 %fusion = f32[64,1024]{1,0:T(8,128)} fusion(bf16[1024,1024]{1,0:T(8,128)(2,1)} %param.13, bf16[64,1024]{1,0:T(8,128)(2,1)S(1)} %get-tuple-element.10), kind=kOutput, calls=%fused_computation.3 | convolution fusion | flops 134217728 | bytes 2490368 | tf_op jit(solution)/shard_map/dot_general | solution.py:42
  226.9 0.0 reduce-scatter.2.cloned.1.call-update
  226.9 2.1 multiply_reduce_fusion
  229.0 32.7 %all-reduce = (f32[1024]{0:T(1024)S(1)}, f32[64]{0:T(128)S(1)}) all-reduce(f32[1024]{0:T(1024)S(1)} %multiply_reduce_fusion, f32[64]{0:T(128)S(1)} %get-tuple-element.9), channel_id=1, replica_groups=mesh['bank'=64,'tp'=4] {'tp'}, use_global_device_ids=true, to_apply=%region_6.0 | all-reduce | flops 1088 | bytes 8704 | tf_op jit(solution)/shard_map/psum | solution.py:37
  261.7 0.1 rsqrt_multiply_fusion
  261.8 4.1 %reduce-scatter.2.cloned.1.call-done = f32[16,1024]{1,0:T(8,128)} async-done(((f32[64,1024]{1,0:T(8,128)}), f32[16,1024]{1,0:T(8,128)}) %reduce-scatter.2.cloned.1.call-update) | async-done | bytes 65552 | tf_op jit(solution)/shard_map/reduce_scatter | solution.py:41
  265.9 1.5 multiply_multiply_fusion
  (3 shorter events, 0.0 us)
Async XLA Ops:
  6.5 1.6 copy-start
  6.5 4.0 %copy-start.1 = (bf16[64,3584]{1,0:T(8,128)(2,1)S(1)}, bf16[64,3584]{1,0:T(8,128)(2,1)}, u32[]{:S(2)}) copy-start(bf16[64,3584]{1,0:T(8,128)(2,1)} %param.9) | copy-start | bytes 1376260
  6.5 57.3 %all-reduce.4.cloned.1.call-start = ((), (), s32[]{:S(2)}) async-start(), calls=%async_computation.2 | async-start | bytes 1048576 | tf_op jit(solution)/shard_map/psum | solution.py:18
  10.5 6.2 %copy-start.3 = (s32[128]{0:T(128)S(1)}, s32[128]{0:T(128)}, u32[]{:S(2)}) copy-start(s32[128]{0:T(128)} %param.12) | copy-start | bytes 1540
  10.5 6.5 %copy-start.2 = (s32[2]{0:T(128)S(1)}, s32[2]{0:T(128)}, u32[]{:S(2)}) copy-start(s32[2]{0:T(128)} %param.11) | copy-start | bytes 28
  16.7 249.2 %reduce-scatter.2.cloned.1.call-start = ((), (), s32[]{:S(2)}) async-start(), calls=%async_computation.1 | async-start | bytes 327680 | tf_op jit(solution)/shard_map/reduce_scatter | solution.py:41
Sparse Core Ops, SparseCore 0:
  16.8 47.0 all-reduce.3
  227.1 38.8 reduce-scatter.1
where the time goes:
time: 275 us; the launch traced here: 274 us
  blocking collectives  190 us (69%)
  waiting for transfers between devices  50.9 us (19%)
  between operations  13.5 us (5%)
  matrix products  12.6 us (5%)
  local copies, waits for them, and re-layouts  3.99 us (1%)
  other arithmetic  3.78 us (1%)
    all_gather x1, blocking collectives, per_device(): all_grads = lax.all_gather(grads, 'bank', axis=0, tiled=True)  157 us
    psum x1, waiting for transfers between devices, per_device(): in_all, out_all = lax.psum((in_part, out_part), 'tp')  46.7 us
    psum x1, blocking collectives, per_device(): query_sq, bank_sq = lax.psum((query_part, bank_part), 'tp')  32.7 us
    dot_general x1, matrix products, per_device(): jnp.einsum('rf,tf->rt', proj_in, tok_rows, preferred_element_type=jnp.flo...  6.13 us
  transfers between devices with their start and end apart: 2, of which 2 were waited for; matrix products, arithmetic and copies ran while one was open for 1% of the time, Pallas kernels for 0%

commit v1 on v0

v1 whole, which is shorter than its diff:
```python
import jax
import jax.numpy as jnp
from jax import lax
from jax.experimental import pallas as pl
from jax.experimental.pallas import tpu as pltpu
from jax.sharding import PartitionSpec as P

EPS = 1e-06
MESH = pl.DeviceIdType.MESH
F32, BF16 = jnp.float32, jnp.bfloat16
NX, NY, NZ = 4, 4, 8
TOK = 256
HI = lax.Precision.HIGHEST
NT = (((1,), (1,)), ((), ()))
ORDER = (0, 1, 7, 2, 6, 3, 5, 4)
FAR = (4, 3, 5, 2, 6, 1, 7, 0)
LAG = 3


def kernel(
    len_hbm, perm_hbm, hid, og, pin, pout, bank, out_ref,
    len_s, perm_s, slot_s, win, wout, hbuf, obuf, bbuf, xbuf, xsend, r1, r2, r3,
    gsc, tbuf, r4, tsum, gb, qf, qsb, qr, dbuf, dr, btile, br, sqb,
    ld_sem, h_sem, o_sem, x_ss, x_rs, g_ss, g_rs, ys_ss, ys_rs, yr_ss, yr_rs,
    b_ss, b_rs, q_ss, q_rs, d_ss, d_rs,
):
    b, k = lax.axis_index("bank"), lax.axis_index("tp")
    xh, z, y = b // (NZ * NY), (b // NY) % NZ, b % NY
    xl, c = k // 2, k % 2
    x = xh * 2 + xl

    def dev(xx, yy, zz, cc):
        return ((xx // 2) * (NZ * NY) + zz * NY + yy, (xx % 2) * 2 + cc)

    tp_of = {1: xl * 2 + 1 - c, 2: (1 - xl) * 2 + c, 3: (1 - xl) * 2 + 1 - c}

    owners = ((1 - xl, 1 - c), (1 - xl, c), (xl, 1 - c), (xl, c))
    loads = []

    def load(src, dst, sem):
        cp = pltpu.make_async_copy(src, dst, sem)
        cp.start()
        return cp

    cp_pout = load(pout, wout.at[pl.ds(64, 64)], ld_sem.at[1])
    cp_pin = load(pin, win.at[pl.ds(0, 64)], ld_sem.at[0])
    for s, (xo, co) in enumerate(owners):
        rows = pl.ds(pl.multiple_of(co * TOK, TOK), TOK)
        loads.append(
            (
                load(og.at[xo, rows], obuf.at[s], o_sem.at[s]),
                load(hid.at[xo, rows], hbuf.at[s], h_sem.at[s]),
            )
        )
    cp_len = load(len_hbm, len_s, ld_sem.at[2])
    cp_perm = load(perm_hbm, perm_s, ld_sem.at[3])
    cp_bank = load(bank, bbuf, ld_sem.at[4])

    barrier = pltpu.get_barrier_semaphore()
    peers = []
    for dz in range(NZ):
        for dx in range(NX):
            if dx or dz:
                peers.append(dev((x + dx) % NX, y, (z + dz) % NZ, c))
    peers.append(dev(x, (y + 1) % NY, z, c))
    peers.append(dev(x, (y + NY - 1) % NY, z, c))
    peers.append((b, tp_of[1]))
    peers.append((b, tp_of[3]))
    for peer in peers:
        pl.semaphore_signal(barrier, inc=1, device_id=peer, device_id_type=MESH)

    win[pl.ds(64, 64), :] = jnp.zeros((64, win.shape[1]), BF16)
    wout[pl.ds(0, 64), :] = jnp.zeros((64, wout.shape[1]), BF16)
    cp_pout.wait()
    cp_pin.wait()

    def send(src, dst, ss, rs, to):
        cp = pltpu.make_async_remote_copy(
            src_ref=src, dst_ref=dst, send_sem=ss, recv_sem=rs, device_id=to, device_id_type=MESH
        )
        cp.start()
        return cp

    sent = []

    def factors(s):
        loads[s][0].wait()
        loads[s][1].wait()
        part = lax.dot_general(obuf[s], wout[...], NT, preferred_element_type=F32)
        return part + lax.dot_general(hbuf[s], win[...], NT, preferred_element_type=F32)

    xbuf[0] = factors(0)
    pl.semaphore_wait(barrier, len(peers))
    c1 = send(xbuf.at[0], r1, x_ss.at[0], x_rs.at[0], (b, tp_of[1]))
    xbuf[1] = factors(1)
    c1.wait_recv()
    xsend[...] = xbuf[1] + r1[...]
    c2 = send(xsend, r2, x_ss.at[1], x_rs.at[1], (b, tp_of[2]))
    xbuf[2] = factors(2)
    c3 = send(xbuf.at[2], r3, x_ss.at[2], x_rs.at[2], (b, tp_of[1]))
    own = factors(3)
    cp_len.wait()
    cp_perm.wait()
    c3.wait_recv()
    own = own + r3[...]
    c2.wait_recv()
    own = own + r2[...]
    sent += [c1, c2, c3]

    pos = lax.broadcasted_iota(jnp.int32, (TOK, 128), 0) + c * TOK
    lane = lax.broadcasted_iota(jnp.int32, (TOK, 128), 1)
    live = jnp.where(pos < len_s[xl], own, 0.0)
    twice = jnp.where(lane < 64, pltpu.roll(own, 64, axis=1), own)
    gsc[...] = jnp.dot(jnp.transpose(live)[0:64], twice, precision=HI, preferred_element_type=F32)
    even, odd = gsc[pl.ds(0, 32, stride=2), :], gsc[pl.ds(1, 32, stride=2), :]
    tiles = jnp.where(lane[0:32] < 64, even, odd)
    for to_x in range(2):
        for to_c in range(2):
            share = to_x * 2 + to_c
            tbuf[to_c, to_x] = tiles[8 * share : 8 * share + 8]
    c4 = send(tbuf.at[1 - c], r4, x_ss.at[3], x_rs.at[3], (b, tp_of[1]))
    c4.wait_recv()
    sent.append(c4)
    tsum[...] = tbuf[c] + r4[...]
    mine = y * (NZ * NX) + z * NX + x
    gb[mine] = tsum[xl]

    plane = {}
    for dz in FAR:
        for dx in (2, 1, 3, 0):
            if dx or dz:
                tx, tz = (x + dx) % NX, (z + dz) % NZ
                plane[dx, dz] = send(
                    tsum.at[tx % 2], gb.at[mine], g_ss.at[dz * NX + dx], g_rs.at[dz * NX + dx], dev(tx, y, tz, c)
                )
    sent += list(plane.values())

    cp_bank.wait()

    def bank_rows(i, carry):
        rows = pl.ds(pl.multiple_of(i * 128, 128), 128)
        acc = jnp.zeros((128, 128), F32)
        for j in range(8):
            v = bbuf[rows, pl.ds(128 * j, 128)].astype(F32)
            acc = acc + v * v
        sqb[rows, :] = acc
        return carry

    lax.fori_loop(0, 8, bank_rows, 0)
    sums = lax.dot_general(jnp.ones((8, 128), F32), sqb[...], NT, precision=HI, preferred_element_type=F32)
    sub = lax.broadcasted_iota(jnp.int32, (8, 128), 0)
    tile = jnp.zeros((8, 128), F32)
    for j in range(8):
        tile = jnp.where(sub == j, sums[:, 128 * j : 128 * j + 128], tile)
    btile[...] = tile
    bcp = {r: send(btile, br.at[r - 1], b_ss.at[r - 1], b_rs.at[r - 1], (b, tp_of[r])) for r in (1, 2, 3)}

    def slots(i, carry):
        e = perm_s[i]
        slot_s[i] = ((e // 2) % 4) * (NZ * NX) + ((e // 8) % 8) * NX + (e // 64) * 2 + e % 2
        return carry

    lax.fori_loop(0, 128, slots, 0)

    up, down = dev(x, (y + 1) % NY, z, c), dev(x, (y + NY - 1) % NY, z, c)

    def group(yy, dz):
        return gb.at[pl.ds(((yy + NY) % NY) * (NZ * NX) + ((z - dz + NZ) % NZ) * NX, NX)]

    near_up, near_down, far = {}, {}, {}

    def relay(dz):
        i = ORDER.index(dz)
        if i % 2 == 0:
            near_up[dz].wait_recv()
            far[dz] = send(group(y - 1, dz), group(y - 1, dz), yr_ss.at[dz], yr_rs.at[dz], up)
        else:
            near_down[dz].wait_recv()
            far[dz] = send(group(y + 1, dz), group(y + 1, dz), yr_ss.at[dz], yr_rs.at[dz], down)

    for i, dz in enumerate(ORDER):
        for dx in range(NX):
            if dx or dz:
                plane[dx, dz].wait_recv()
        near_up[dz] = send(group(y, dz), group(y, dz), ys_ss.at[dz], ys_rs.at[dz], up)
        near_down[dz] = send(group(y, dz), group(y, dz), ys_ss.at[8 + dz], ys_rs.at[8 + dz], down)
        if i >= LAG:
            relay(ORDER[i - LAG])
    for dz in ORDER[len(ORDER) - LAG :]:
        relay(dz)
    for i, dz in enumerate(ORDER):
        (near_down if i % 2 == 0 else near_up)[dz].wait_recv()
    for dz in ORDER:
        far[dz].wait_recv()
    sent += list(near_up.values()) + list(near_down.values()) + list(far.values())

    def query(p, carry):
        rows = pl.ds(pl.multiple_of(p * 8, 8), 8)
        qf[rows, :] = gb[slot_s[2 * p + 1]] - gb[slot_s[2 * p]]
        return carry

    lax.fori_loop(0, 64, query, 0, unroll=8)
    cols, acc = [], jnp.zeros((64, 128), F32)
    for v in range(8):
        part = qf[pl.ds(v, 64, stride=8), :]
        acc = acc + part * part
        cols.append(part.astype(BF16))
    low = jnp.concatenate(cols, axis=1)
    qsq = jnp.broadcast_to(jnp.sum(acc, axis=1, keepdims=True), (64, 128))
    for s in range(4):
        qsb[s] = qsq[16 * s : 16 * s + 16]
    qcp = {r: send(qsb.at[tp_of[r]], qr.at[r - 1], q_ss.at[r - 1], q_rs.at[r - 1], (b, tp_of[r])) for r in (2, 3, 1)}
    dcp = {}
    for j in range(4):
        part = lax.dot_general(low, bbuf[pl.ds(256 * j, 256), :], NT, preferred_element_type=F32)
        for s in range(4):
            dbuf[j, s] = part[16 * s : 16 * s + 16]
        for r in (2, 3, 1):
            dcp[j, r] = send(
                dbuf.at[j, tp_of[r]], dr.at[j, r - 1], d_ss.at[j * 3 + r - 1], d_rs.at[j * 3 + r - 1], (b, tp_of[r])
            )
    for r in (1, 2, 3):
        bcp[r].wait_recv()
    norms = lax.rsqrt(btile[...] + br[0] + br[1] + br[2] + EPS)
    for r in (1, 2, 3):
        qcp[r].wait_recv()
    scale = lax.rsqrt(qsb[k] + qr[0] + qr[1] + qr[2] + EPS) * 64.0
    for j in range(4):
        for r in (1, 2, 3):
            dcp[j, r].wait_recv()
        for h in range(2):
            cs = pl.ds(128 * h, 128)
            total = dbuf[j, k, :, cs] + dr[j, 0, :, cs] + dr[j, 1, :, cs] + dr[j, 2, :, cs]
            n = 2 * j + h
            out_ref[:, pl.ds(128 * n, 128)] = total * scale * norms[n : n + 1, :]
    sent += list(bcp.values()) + list(qcp.values()) + list(dcp.values())
    for cp in sent:
        cp.wait_send()


def per_device(hidden, out_grad, proj_in, proj_out, lengths, pair_perm, bank_slab):
    ff, d = hidden.shape[2], out_grad.shape[2]
    any_spec = pl.BlockSpec(memory_space=pl.ANY)
    V, D = pltpu.VMEM, pltpu.SemaphoreType.DMA
    return pl.pallas_call(
        kernel,
        out_shape=jax.ShapeDtypeStruct((16, 1024), F32),
        in_specs=[any_spec] * 7,
        out_specs=pl.BlockSpec(memory_space=pltpu.VMEM),
        scratch_shapes=[
            pltpu.SMEM((2,), jnp.int32),
            pltpu.SMEM((128,), jnp.int32),
            pltpu.SMEM((128,), jnp.int32),
            V((128, ff), BF16),
            V((128, d), BF16),
            V((4, TOK, ff), BF16),
            V((4, TOK, d), BF16),
            V((1024, 1024), BF16),
            V((3, TOK, 128), F32),
            V((TOK, 128), F32),
            V((TOK, 128), F32),
            V((TOK, 128), F32),
            V((TOK, 128), F32),
            V((64, 128), F32),
            V((2, 2, 8, 128), F32),
            V((2, 8, 128), F32),
            V((2, 8, 128), F32),
            V((128, 8, 128), F32),
            V((512, 128), F32),
            V((4, 16, 128), F32),
            V((3, 16, 128), F32),
            V((4, 4, 16, 256), F32),
            V((4, 3, 16, 256), F32),
            V((8, 128), F32),
            V((3, 8, 128), F32),
            V((1024, 128), F32),
            D((5,)),
            D((4,)),
            D((4,)),
            D((4,)),
            D((4,)),
            D((32,)),
            D((32,)),
            D((16,)),
            D((16,)),
            D((8,)),
            D((8,)),
            D((3,)),
            D((3,)),
            D((3,)),
            D((3,)),
            D((12,)),
            D((12,)),
        ],
        compiler_params=pltpu.CompilerParams(
            collective_id=0, has_side_effects=True, vmem_limit_bytes=60 * 1024 * 1024
        ),
    )(lengths, pair_perm, hidden, out_grad, proj_in, proj_out, bank_slab)


def solution(mesh):
    return jax.shard_map(
        per_device,
        mesh=mesh,
        in_specs=(
            P("bank", None, "tp"),
            P("bank", None, "tp"),
            P(None, "tp"),
            P(None, "tp"),
            P("bank"),
            P(),
            P("bank", "tp"),
        ),
        out_specs=P("tp", "bank"),
        check_vma=False,
    )
```

time: 275 us -> 42 us (0.15)
  blocking collectives: 190 us -> 0 us
  waiting for transfers between devices: 50.9 us -> 0 us
  Pallas kernels: 0 us -> 40.4 us
  between operations: 13.5 us -> 0.01 us
  matrix products: 12.6 us -> 0 us
  other arithmetic: 3.78 us -> 0 us
    all_gather x1 -> x0, blocking collectives: 157 us -> none  [per_device(): all_grads = lax.all_gather(grads, 'bank', axis=0, tiled=True)]
    psum x1 -> x0, waiting for transfers between devices: 46.7 us -> none  [per_device(): in_all, out_all = lax.psum((in_part, out_part), 'tp')]
    pallas_call x0 -> x1, Pallas kernels: none -> 40.4 us  [per_device(): pl.pallas_call(kernel, out_shape=jax.ShapeDtypeStruct((16, 1024), F32), i...]
    psum x1 -> x0, blocking collectives: 32.7 us -> none  [per_device(): query_sq, bank_sq = lax.psum((query_part, bank_part), 'tp')]
    dot_general x5 -> x0, matrix products: 12.6 us -> none  [the longest x1 6.13 us: per_device(): jnp.einsum('rf,tf->rt', proj_in, tok_rows, preferred_element_type=jnp.flo...]
    reduce_scatter x1 -> x0, waiting for transfers between devices: 4.13 us -> none  [per_device(): lax.psum_scatter(lax.dot_general(query_low, bank_slab, (((1,), (1,)), (()...]
  transfers between devices with their start and end apart: 2 -> 0, of which waited for: 2 -> 0; matrix products, arithmetic and copies ran while one was open for 1% -> 0% of each run, Pallas kernels for 0% -> 0%
where the time goes in v1:
time: 42 us; the launch traced here: 41.9 us
  Pallas kernels  40.4 us (96%)
  local copies, waits for them, and re-layouts  1.47 us (4%)
    pallas_call x1, Pallas kernels, per_device(): pl.pallas_call(kernel, out_shape=jax.ShapeDtypeStruct((16, 1024), F32), i...  40.4 us
    unnamed x1, local copies, waits for them, and re-layouts  1.47 us

profile of v1, /device:TPU:1, one launch (start us, length us, event | category | flops | bytes accessed | tf_op | source)
XLA Modules:
  0.0 41.9 jit_solution(14906205326862162466)
XLA Ops:
  0.0 40.4 %shard_map.73 = f32[16,1024]{1,0:T(8,128)} custom-call(s32[2]{0:T(128)} %len_hbm.1, s32[128]{0:T(128)} %perm_hbm.1, bf16[2,512,3584]{2,1,0:T(8,128)(2,1)} %hid.1, bf16[2,512,1024]{2,1,0:T(8,128)(2,1)} %og.1, bf16[64,3584]{1,0:T(8,128)(2,1)} %pin.1, bf16[64,1024]{1,0:T(8,128)(2,1)} %pout.1, bf16[1024,1024]{1,0:T(8,128)(2,1)} %bank.1), custom_call_target="tpu_custom_call" | custom-call | tf_op jit(solution)/shard_map/pallas_call | solution.py:245
  40.4 1.5 %copy.9 = f32[16,1024]{1,0:T(8,128)} copy(f32[16,1024]{1,0:T(8,128)} %shard_map.73) | data formatting | bytes 131072

commit v2 on v1

v2 whole, which is shorter than its diff:
```python
import jax
import jax.numpy as jnp
from jax import lax
from jax.experimental import pallas as pl
from jax.experimental.pallas import tpu as pltpu
from jax.sharding import PartitionSpec as P

EPS = 1e-06
MESH = pl.DeviceIdType.MESH
F32, BF16 = jnp.float32, jnp.bfloat16
NX, NY, NZ = 4, 4, 8
TOK = 256
HI = lax.Precision.HIGHEST
NT = (((1,), (1,)), ((), ()))
EARLY, LATE = (0, 1, 2, 3), (7, 4, 6, 5)
GROUPS = (0, 1, 2, 3, 7, 6, 5, 4)


def kernel(
    len_hbm, perm_hbm, hid, og, pin, pout, bank, out_ref,
    len_s, perm_s, slot_s, win, wout, hbuf, obuf, bbuf, part, total, ra, rc, rx,
    gsc, tbuf, r4, tsum, gb, qf, qsb, qr, dbuf, dr, btile, br, sqb,
    ld_sem, h_sem, o_sem, x_ss, x_rs, g_ss, g_rs, y_ss, y_rs, ready,
    b_ss, b_rs, q_ss, q_rs, d_ss, d_rs,
):
    b, k = lax.axis_index("bank"), lax.axis_index("tp")
    xh, z, y = b // (NZ * NY), (b // NY) % NZ, b % NY
    xl, c = k // 2, k % 2
    x = xh * 2 + xl

    def dev(xx, yy, zz, cc):
        return ((xx // 2) * (NZ * NY) + zz * NY + yy, (xx % 2) * 2 + cc)

    tp_of = {1: xl * 2 + 1 - c, 2: (1 - xl) * 2 + c, 3: (1 - xl) * 2 + 1 - c}

    owners = ((1 - xl, c), (1 - xl, 1 - c), (xl, 1 - c), (xl, c))

    def load(src, dst, sem):
        cp = pltpu.make_async_copy(src, dst, sem)
        cp.start()
        return cp

    def block(s):
        xo, co = owners[s]
        return xo, pl.ds(pl.multiple_of(co * TOK, TOK), TOK)

    def load_og(s):
        return load(og.at[block(s)], obuf.at[s], o_sem.at[s])

    def load_hid(s):
        return load(hid.at[block(s)], hbuf.at[s], h_sem.at[s])

    cp_pout = load(pout, wout.at[0, pl.ds(0, 64)], ld_sem.at[1])
    ogs = [load_og(0), load_og(1)]
    cp_pin = load(pin, win.at[0, pl.ds(0, 64)], ld_sem.at[0])
    hids = [load_hid(0)]

    barrier = pltpu.get_barrier_semaphore()

    def greet(sem, to):
        pl.semaphore_signal(sem, inc=1, device_id=to, device_id_type=MESH)

    for r in (1, 2, 3):
        greet(barrier, (b, tp_of[r]))
    for zz in range(NZ):
        for xx in range(NX):

            @pl.when(jnp.logical_or(zz > z, jnp.logical_and(zz == z, xx // 2 > xh)))
            def _(zz=zz, xx=xx):
                greet(barrier, dev(xx, y, zz, c))

    for yy in range(1, NY):

        @pl.when(yy > y)
        def _(yy=yy):
            greet(barrier, dev(x, yy, z, c))

    def greet_back():
        for zz in range(NZ):

            @pl.when(jnp.logical_and(xh == 1, jnp.logical_or(zz < z, jnp.logical_and(zz == z, xl == 0))))
            def _(zz=zz):
                for dx in range(2):
                    greet(ready.at[z], dev(2 * xl + dx, y, zz, c))

        for yy in range(NY - 1):

            @pl.when(yy < y)
            def _(yy=yy):
                greet(ready.at[NZ], dev(x, yy, z, c))

    for w in (win, wout):
        w[0, pl.ds(64, 64)] = jnp.zeros((64, w.shape[2]), BF16)
        w[1, pl.ds(0, 64)] = jnp.zeros((64, w.shape[2]), BF16)

    def send(src, dst, ss, rs, to):
        cp = pltpu.make_async_remote_copy(
            src_ref=src, dst_ref=dst, send_sem=ss, recv_sem=rs, device_id=to, device_id_type=MESH
        )
        cp.start()
        return cp

    sent = []

    def packed(rows, s, w):
        low = lax.dot_general(rows[s, pl.ds(0, 128)], w[0], NT, preferred_element_type=F32)
        return low + lax.dot_general(rows[s, pl.ds(128, 128)], w[1], NT, preferred_element_type=F32)

    pair, cross = (b, tp_of[1]), (b, tp_of[3])
    cp_pout.wait()
    wout[1, pl.ds(64, 64)] = wout[0, pl.ds(0, 64)]
    ogs[0].wait()
    hids.append(load_hid(1))
    part[0, 0] = packed(obuf, 0, wout)
    pl.semaphore_wait(barrier, 3 + NX * z + 2 * xh + y)
    greet_back()
    ca = [send(part.at[0, 0], ra.at[0], x_ss.at[0], x_rs.at[0], pair)]
    ogs[1].wait()
    out_b = packed(obuf, 1, wout)
    cp_pin.wait()
    win[1, pl.ds(64, 64)] = win[0, pl.ds(0, 64)]
    hids[0].wait()
    ogs += [load_og(2), load_og(3)]
    hids.append(load_hid(2))
    part[0, 1] = packed(hbuf, 0, win)
    ca.append(send(part.at[0, 1], ra.at[1], x_ss.at[1], x_rs.at[1], pair))
    ca[0].wait_recv()
    total[0] = out_b + ra[0]
    cx = [send(total.at[0], rx.at[0], x_ss.at[2], x_rs.at[2], cross)]
    hids[1].wait()
    hids.append(load_hid(3))
    in_b = packed(hbuf, 1, win)
    ca[1].wait_recv()
    total[1] = in_b + ra[1]
    cx.append(send(total.at[1], rx.at[1], x_ss.at[3], x_rs.at[3], cross))
    cp_len = load(len_hbm, len_s, ld_sem.at[2])
    cp_perm = load(perm_hbm, perm_s, ld_sem.at[3])
    cp_bank = load(bank, bbuf, ld_sem.at[4])
    ogs[2].wait()
    part[1, 0] = packed(obuf, 2, wout)
    cc = [send(part.at[1, 0], rc.at[0], x_ss.at[4], x_rs.at[4], pair)]
    hids[2].wait()
    part[1, 1] = packed(hbuf, 2, win)
    cc.append(send(part.at[1, 1], rc.at[1], x_ss.at[5], x_rs.at[5], pair))
    ogs[3].wait()
    out_d = packed(obuf, 3, wout)
    hids[3].wait()
    in_d = packed(hbuf, 3, win)
    cp_len.wait()
    cp_perm.wait()
    cc[0].wait_recv()
    cx[0].wait_recv()
    out_d = out_d + rc[0] + rx[0]
    cc[1].wait_recv()
    in_d = in_d + rc[1]
    cx[1].wait_recv()
    in_d = in_d + rx[1]
    sent += ca + cx + cc

    lane = lax.broadcasted_iota(jnp.int32, (128, 128), 1)
    pos = lax.broadcasted_iota(jnp.int32, (128, 128), 0) + jnp.where(lane < 64, 0, 128) + c * TOK
    live = jnp.where(pos < len_s[xl], in_d, 0.0)
    outer = jnp.dot(jnp.transpose(live), out_d, precision=HI, preferred_element_type=F32)
    halves = jnp.where(lane[0:64] < 64, outer[0:64], outer[64:128])
    gsc[...] = halves + pltpu.roll(halves, 64, axis=1)
    even, odd = gsc[pl.ds(0, 32, stride=2), :], gsc[pl.ds(1, 32, stride=2), :]
    tiles = jnp.where(lane[0:32] < 64, even, odd)
    for to_x in range(2):
        for to_c in range(2):
            share = to_x * 2 + to_c
            tbuf[to_c, to_x] = tiles[8 * share : 8 * share + 8]
    c4 = send(tbuf.at[1 - c], r4, x_ss.at[6], x_rs.at[6], pair)
    c4.wait_recv()
    sent.append(c4)
    tsum[...] = tbuf[c] + r4[...]
    mine = y * (NZ * NX) + z * NX + x
    gb[mine] = tsum[xl]

    def plane_copy(tx, tz, slot):
        return pltpu.make_async_remote_copy(
            src_ref=tsum.at[tx % 2], dst_ref=gb.at[mine], send_sem=g_ss.at[slot], recv_sem=g_rs.at[z * NX + x],
            device_id=dev(tx, y, tz, c), device_id_type=MESH,
        )

    def to_rows(rows):
        for tz in rows:

            @pl.when(jnp.logical_or(tz > z, jnp.logical_and(tz == z, xh == 0)))
            def _(tz=tz):
                pl.semaphore_wait(ready.at[tz], 1)

            for dx in (2, 1, 3):
                plane_copy((x + dx) % NX, tz, tz * NX + dx).start()

            @pl.when(tz != z)
            def _(tz=tz):
                plane_copy(x, tz, tz * NX).start()

    to_rows(EARLY)

    @pl.when(z >= 4)
    def _():
        to_rows(LATE)

    cp_bank.wait()

    def bank_rows(i, carry):
        rows = pl.ds(pl.multiple_of(i * 128, 128), 128)
        acc = jnp.zeros((128, 128), F32)
        for j in range(8):
            v = bbuf[rows, pl.ds(128 * j, 128)].astype(F32)
            acc = acc + v * v
        sqb[rows, :] = acc
        return carry

    lax.fori_loop(0, 8, bank_rows, 0)
    sums = lax.dot_general(jnp.ones((8, 128), F32), sqb[...], NT, precision=HI, preferred_element_type=F32)
    sub = lax.broadcasted_iota(jnp.int32, (8, 128), 0)
    tile = jnp.zeros((8, 128), F32)
    for j in range(8):
        tile = jnp.where(sub == j, sums[:, 128 * j : 128 * j + 128], tile)
    btile[...] = tile
    bcp = {r: send(btile, br.at[r - 1], b_ss.at[r - 1], b_rs.at[r - 1], (b, tp_of[r])) for r in (1, 2, 3)}

    def slots(i, carry):
        e = perm_s[i]
        slot_s[i] = ((e // 2) % 4) * (NZ * NX) + ((e // 8) % 8) * NX + (e // 64) * 2 + e % 2
        return carry

    lax.fori_loop(0, 128, slots, 0)

    up, down = dev(x, (y + 1) % NY, z, c), dev(x, (y + NY - 1) % NY, z, c)

    def group(yy, zz):
        return gb.at[pl.ds(((yy + NY) % NY) * (NZ * NX) + zz * NX, NX)]

    def plane_wait(zz, xx):
        pltpu.make_async_remote_copy(
            src_ref=tsum.at[0], dst_ref=gb.at[mine], send_sem=g_ss.at[0], recv_sem=g_rs.at[zz * NX + xx],
            device_id=up, device_id_type=MESH,
        ).wait_recv()

    across = dev(x, (y + 2) % NY, z, c)
    along = []

    @pl.when(y < NY - 1)
    def _():
        pl.semaphore_wait(ready.at[NZ], NY - 1 - y)

    for i, zz in enumerate(GROUPS):
        if i == 1:

            @pl.when(z < 4)
            def _():
                to_rows(LATE)

        for xx in range(NX):

            @pl.when(jnp.logical_or(zz != z, xx != x))
            def _(zz=zz, xx=xx):
                plane_wait(zz, xx)

        for n, to in enumerate((across, up, down)):
            slot = n * NZ + zz
            along.append(send(group(y, zz), group(y, zz), y_ss.at[slot], y_rs.at[slot], to))
    for cp in along:
        cp.wait_recv()
    sent += along

    def query(p, carry):
        rows = pl.ds(pl.multiple_of(p * 8, 8), 8)
        qf[rows, :] = gb[slot_s[2 * p + 1]] - gb[slot_s[2 * p]]
        return carry

    lax.fori_loop(0, 64, query, 0, unroll=8)
    cols, acc = [], jnp.zeros((64, 128), F32)
    for v in range(8):
        part = qf[pl.ds(v, 64, stride=8), :]
        acc = acc + part * part
        cols.append(part.astype(BF16))
    low = jnp.concatenate(cols, axis=1)
    qsq = jnp.broadcast_to(jnp.sum(acc, axis=1, keepdims=True), (64, 128))
    for s in range(4):
        qsb[s] = qsq[16 * s : 16 * s + 16]
    qcp = {r: send(qsb.at[tp_of[r]], qr.at[r - 1], q_ss.at[r - 1], q_rs.at[r - 1], (b, tp_of[r])) for r in (2, 3, 1)}
    dcp = {}
    for j in range(4):
        part = lax.dot_general(low, bbuf[pl.ds(256 * j, 256), :], NT, preferred_element_type=F32)
        for s in range(4):
            dbuf[j, s] = part[16 * s : 16 * s + 16]
        for r in (2, 3, 1):
            dcp[j, r] = send(
                dbuf.at[j, tp_of[r]], dr.at[j, r - 1], d_ss.at[j * 3 + r - 1], d_rs.at[j * 3 + r - 1], (b, tp_of[r])
            )
    for r in (1, 2, 3):
        bcp[r].wait_recv()
    norms = lax.rsqrt(btile[...] + br[0] + br[1] + br[2] + EPS)
    for r in (1, 2, 3):
        qcp[r].wait_recv()
    scale = lax.rsqrt(qsb[k] + qr[0] + qr[1] + qr[2] + EPS) * 64.0
    for j in range(4):
        for r in (1, 2, 3):
            dcp[j, r].wait_recv()
        for h in range(2):
            cs = pl.ds(128 * h, 128)
            total = dbuf[j, k, :, cs] + dr[j, 0, :, cs] + dr[j, 1, :, cs] + dr[j, 2, :, cs]
            n = 2 * j + h
            out_ref[:, pl.ds(128 * n, 128)] = total * scale * norms[n : n + 1, :]
    sent += list(bcp.values()) + list(qcp.values()) + list(dcp.values())
    for cp in sent:
        cp.wait_send()
    for tz in EARLY + LATE:
        for dx in (2, 1, 3):
            plane_copy((x + dx) % NX, tz, tz * NX + dx).wait_send()

        @pl.when(tz != z)
        def _(tz=tz):
            plane_copy(x, tz, tz * NX).wait_send()


def per_device(hidden, out_grad, proj_in, proj_out, lengths, pair_perm, bank_slab):
    ff, d = hidden.shape[2], out_grad.shape[2]
    any_spec = pl.BlockSpec(memory_space=pl.ANY)
    V, D = pltpu.VMEM, pltpu.SemaphoreType.DMA
    return pl.pallas_call(
        kernel,
        out_shape=jax.ShapeDtypeStruct((16, 1024), F32),
        in_specs=[any_spec] * 7,
        out_specs=pl.BlockSpec(memory_space=pltpu.VMEM),
        scratch_shapes=[
            pltpu.SMEM((2,), jnp.int32),
            pltpu.SMEM((128,), jnp.int32),
            pltpu.SMEM((128,), jnp.int32),
            V((2, 128, ff), BF16),
            V((2, 128, d), BF16),
            V((4, TOK, ff), BF16),
            V((4, TOK, d), BF16),
            V((1024, 1024), BF16),
            V((2, 2, 128, 128), F32),
            V((2, 128, 128), F32),
            V((2, 128, 128), F32),
            V((2, 128, 128), F32),
            V((2, 128, 128), F32),
            V((64, 128), F32),
            V((2, 2, 8, 128), F32),
            V((2, 8, 128), F32),
            V((2, 8, 128), F32),
            V((128, 8, 128), F32),
            V((512, 128), F32),
            V((4, 16, 128), F32),
            V((3, 16, 128), F32),
            V((4, 4, 16, 256), F32),
            V((4, 3, 16, 256), F32),
            V((8, 128), F32),
            V((3, 8, 128), F32),
            V((1024, 128), F32),
            D((5,)),
            D((4,)),
            D((4,)),
            D((7,)),
            D((7,)),
            D((32,)),
            D((32,)),
            D((24,)),
            D((24,)),
            pltpu.SemaphoreType.REGULAR((NZ + 1,)),
            D((3,)),
            D((3,)),
            D((3,)),
            D((3,)),
            D((12,)),
            D((12,)),
        ],
        compiler_params=pltpu.CompilerParams(
            collective_id=0, has_side_effects=True, vmem_limit_bytes=60 * 1024 * 1024
        ),
    )(lengths, pair_perm, hidden, out_grad, proj_in, proj_out, bank_slab)


def solution(mesh):
    return jax.shard_map(
        per_device,
        mesh=mesh,
        in_specs=(
            P("bank", None, "tp"),
            P("bank", None, "tp"),
            P(None, "tp"),
            P(None, "tp"),
            P("bank"),
            P(),
            P("bank", "tp"),
        ),
        out_specs=P("tp", "bank"),
        check_vma=False,
    )
```

time: 42 us -> 36.1 us (0.86)
  Pallas kernels: 40.4 us -> 34.5 us
    pallas_call x1, Pallas kernels: 40.4 us -> 34.5 us  [per_device(): pl.pallas_call(kernel, out_shape=jax.ShapeDtypeStruct((16, 1024), F32), i...]
where the time goes in v2:
time: 36.1 us; the launch traced here: 36 us
  Pallas kernels  34.5 us (96%)
  local copies, waits for them, and re-layouts  1.47 us (4%)
    pallas_call x1, Pallas kernels, per_device(): pl.pallas_call(kernel, out_shape=jax.ShapeDtypeStruct((16, 1024), F32), i...  34.5 us
    unnamed x1, local copies, waits for them, and re-layouts  1.47 us

profile of v2, /device:TPU:1, one launch (start us, length us, event | category | flops | bytes accessed | tf_op | source)
XLA Modules:
  0.0 36.0 jit_solution(2147652630966744615)
XLA Ops:
  0.0 34.5 %shard_map.73 = f32[16,1024]{1,0:T(8,128)} custom-call(s32[2]{0:T(128)} %len_hbm.1, s32[128]{0:T(128)} %perm_hbm.1, bf16[2,512,3584]{2,1,0:T(8,128)(2,1)} %hid.1, bf16[2,512,1024]{2,1,0:T(8,128)(2,1)} %og.1, bf16[64,3584]{1,0:T(8,128)(2,1)} %pin.1, bf16[64,1024]{1,0:T(8,128)(2,1)} %pout.1, bf16[1024,1024]{1,0:T(8,128)(2,1)} %bank.1), custom_call_target="tpu_custom_call" | custom-call | tf_op jit(solution)/shard_map/pallas_call | solution.py:325
  34.5 1.5 %copy.9 = f32[16,1024]{1,0:T(8,128)} copy(f32[16,1024]{1,0:T(8,128)} %shard_map.73) | data formatting | bytes 131072

commit v3 on v2

--- a/solution.py
+++ b/solution.py
@@ -53,7 +53,7 @@
     cp_pout = load(pout, wout.at[0, pl.ds(0, 64)], ld_sem.at[1])
     ogs = [load_og(0), load_og(1)]
     cp_pin = load(pin, win.at[0, pl.ds(0, 64)], ld_sem.at[0])
-    hids = [load_hid(0)]
+    hids = [load_hid(0), load_hid(1)]
 
     barrier = pltpu.get_barrier_semaphore()
 
@@ -110,7 +110,8 @@
     cp_pout.wait()
     wout[1, pl.ds(64, 64)] = wout[0, pl.ds(0, 64)]
     ogs[0].wait()
-    hids.append(load_hid(1))
+    ogs += [load_og(2), load_og(3)]
+    hids.append(load_hid(2))
     part[0, 0] = packed(obuf, 0, wout)
     pl.semaphore_wait(barrier, 3 + NX * z + 2 * xh + y)
     greet_back()
@@ -120,15 +121,13 @@
     cp_pin.wait()
     win[1, pl.ds(64, 64)] = win[0, pl.ds(0, 64)]
     hids[0].wait()
-    ogs += [load_og(2), load_og(3)]
-    hids.append(load_hid(2))
+    hids.append(load_hid(3))
     part[0, 1] = packed(hbuf, 0, win)
     ca.append(send(part.at[0, 1], ra.at[1], x_ss.at[1], x_rs.at[1], pair))
     ca[0].wait_recv()
     total[0] = out_b + ra[0]
     cx = [send(total.at[0], rx.at[0], x_ss.at[2], x_rs.at[2], cross)]
     hids[1].wait()
-    hids.append(load_hid(3))
     in_b = packed(hbuf, 1, win)
     ca[1].wait_recv()
     total[1] = in_b + ra[1]
@@ -282,7 +281,6 @@
     qsq = jnp.broadcast_to(jnp.sum(acc, axis=1, keepdims=True), (64, 128))
     for s in range(4):
         qsb[s] = qsq[16 * s : 16 * s + 16]
-    qcp = {r: send(qsb.at[tp_of[r]], qr.at[r - 1], q_ss.at[r - 1], q_rs.at[r - 1], (b, tp_of[r])) for r in (2, 3, 1)}
     dcp = {}
     for j in range(4):
         part = lax.dot_general(low, bbuf[pl.ds(256 * j, 256), :], NT, preferred_element_type=F32)
@@ -292,6 +290,7 @@
             dcp[j, r] = send(
                 dbuf.at[j, tp_of[r]], dr.at[j, r - 1], d_ss.at[j * 3 + r - 1], d_rs.at[j * 3 + r - 1], (b, tp_of[r])
             )
+    qcp = {r: send(qsb.at[tp_of[r]], qr.at[r - 1], q_ss.at[r - 1], q_rs.at[r - 1], (b, tp_of[r])) for r in (2, 3, 1)}
     for r in (1, 2, 3):
         bcp[r].wait_recv()
     norms = lax.rsqrt(btile[...] + br[0] + br[1] + br[2] + EPS)

time: 36.1 us -> 36.5 us (1.011)
  Pallas kernels: 34.5 us -> 34.9 us
where the time goes in v3:
time: 36.5 us; the launch traced here: 36.4 us
  Pallas kernels  34.9 us (96%)
  local copies, waits for them, and re-layouts  1.47 us (4%)
    pallas_call x1, Pallas kernels, per_device(): pl.pallas_call(kernel, out_shape=jax.ShapeDtypeStruct((16, 1024), F32), i...  34.9 us
    unnamed x1, local copies, waits for them, and re-layouts  1.47 us

profile of v3, /device:TPU:1, one launch (start us, length us, event | category | flops | bytes accessed | tf_op | source)
XLA Modules:
  0.0 36.4 jit_solution(3706744633068166877)
XLA Ops:
  0.0 34.9 %shard_map.73 = f32[16,1024]{1,0:T(8,128)} custom-call(s32[2]{0:T(128)} %len_hbm.1, s32[128]{0:T(128)} %perm_hbm.1, bf16[2,512,3584]{2,1,0:T(8,128)(2,1)} %hid.1, bf16[2,512,1024]{2,1,0:T(8,128)(2,1)} %og.1, bf16[64,3584]{1,0:T(8,128)(2,1)} %pin.1, bf16[64,1024]{1,0:T(8,128)(2,1)} %pout.1, bf16[1024,1024]{1,0:T(8,128)(2,1)} %bank.1), custom_call_target="tpu_custom_call" | custom-call | tf_op jit(solution)/shard_map/pallas_call | solution.py:324
  34.9 1.5 %copy.9 = f32[16,1024]{1,0:T(8,128)} copy(f32[16,1024]{1,0:T(8,128)} %shard_map.73) | data formatting | bytes 131072

commit v4 on v2

--- a/solution.py
+++ b/solution.py
@@ -284,8 +284,8 @@
         qsb[s] = qsq[16 * s : 16 * s + 16]
     qcp = {r: send(qsb.at[tp_of[r]], qr.at[r - 1], q_ss.at[r - 1], q_rs.at[r - 1], (b, tp_of[r])) for r in (2, 3, 1)}
     dcp = {}
-    for j in range(4):
-        part = lax.dot_general(low, bbuf[pl.ds(256 * j, 256), :], NT, preferred_element_type=F32)
+    for j in range(8):
+        part = lax.dot_general(low, bbuf[pl.ds(128 * j, 128), :], NT, preferred_element_type=F32)
         for s in range(4):
             dbuf[j, s] = part[16 * s : 16 * s + 16]
         for r in (2, 3, 1):
@@ -298,14 +298,11 @@
     for r in (1, 2, 3):
         qcp[r].wait_recv()
     scale = lax.rsqrt(qsb[k] + qr[0] + qr[1] + qr[2] + EPS) * 64.0
-    for j in range(4):
+    for j in range(8):
         for r in (1, 2, 3):
             dcp[j, r].wait_recv()
-        for h in range(2):
-            cs = pl.ds(128 * h, 128)
-            total = dbuf[j, k, :, cs] + dr[j, 0, :, cs] + dr[j, 1, :, cs] + dr[j, 2, :, cs]
-            n = 2 * j + h
-            out_ref[:, pl.ds(128 * n, 128)] = total * scale * norms[n : n + 1, :]
+        dots = dbuf[j, k] + dr[j, 0] + dr[j, 1] + dr[j, 2]
+        out_ref[:, pl.ds(128 * j, 128)] = dots * scale * norms[j : j + 1, :]
     sent += list(bcp.values()) + list(qcp.values()) + list(dcp.values())
     for cp in sent:
         cp.wait_send()
@@ -349,8 +346,8 @@
             V((512, 128), F32),
             V((4, 16, 128), F32),
             V((3, 16, 128), F32),
-            V((4, 4, 16, 256), F32),
-            V((4, 3, 16, 256), F32),
+            V((8, 4, 16, 128), F32),
+            V((8, 3, 16, 128), F32),
             V((8, 128), F32),
             V((3, 8, 128), F32),
             V((1024, 128), F32),
@@ -368,8 +365,8 @@
             D((3,)),
             D((3,)),
             D((3,)),
-            D((12,)),
-            D((12,)),
+            D((24,)),
+            D((24,)),
         ],
         compiler_params=pltpu.CompilerParams(
             collective_id=0, has_side_effects=True, vmem_limit_bytes=60 * 1024 * 1024

time: 36.1 us -> 36.8 us (1.019)
  Pallas kernels: 34.5 us -> 35.2 us
    pallas_call x1, Pallas kernels: 34.5 us -> 35.2 us  [per_device(): pl.pallas_call(kernel, out_shape=jax.ShapeDtypeStruct((16, 1024), F32), i...]
where the time goes in v4:
time: 36.8 us; the launch traced here: 36.6 us
  Pallas kernels  35.2 us (96%)
  local copies, waits for them, and re-layouts  1.47 us (4%)
    pallas_call x1, Pallas kernels, per_device(): pl.pallas_call(kernel, out_shape=jax.ShapeDtypeStruct((16, 1024), F32), i...  35.2 us
    unnamed x1, local copies, waits for them, and re-layouts  1.47 us

profile of v4, /device:TPU:1, one launch (start us, length us, event | category | flops | bytes accessed | tf_op | source)
XLA Modules:
  0.0 36.6 jit_solution(10648594641613984138)
XLA Ops:
  0.0 35.2 %shard_map.73 = f32[16,1024]{1,0:T(8,128)} custom-call(s32[2]{0:T(128)} %len_hbm.1, s32[128]{0:T(128)} %perm_hbm.1, bf16[2,512,3584]{2,1,0:T(8,128)(2,1)} %hid.1, bf16[2,512,1024]{2,1,0:T(8,128)(2,1)} %og.1, bf16[64,3584]{1,0:T(8,128)(2,1)} %pin.1, bf16[64,1024]{1,0:T(8,128)(2,1)} %pout.1, bf16[1024,1024]{1,0:T(8,128)(2,1)} %bank.1), custom_call_target="tpu_custom_call" | custom-call | tf_op jit(solution)/shard_map/pallas_call | solution.py:322
  35.2 1.5 %copy.9 = f32[16,1024]{1,0:T(8,128)} copy(f32[16,1024]{1,0:T(8,128)} %shard_map.73) | data formatting | bytes 131072
